TPU v7x, 256 devices: a whole 4x4x8 slice. The times are simulated.
256 devices in a mesh: az: 32 (over x, z_hi, core), rad: 8 (over z_lo, y).
Axes of the slice: x: 4, y: 4, z: 8 (z_hi: 4, z_lo: 2; z = z_hi * 2 + z_lo), core: 2. Of those that a mesh axis runs over, the one named last changes fastest.
Arguments:
- fields: float32 [5, 8, 512, 4096], P(None, None, 'rad', 'az'), may hold values from -6 to 6
- velocity: float32 [8, 512, 4096], P(None, 'rad', 'az'), may hold values from -0.5 to 0.5
- shifts: int32 [512], P('rad'), may hold values from 0 to 4095, as said below
- block_inverse: float32 [8, 512, 64], P(None, 'rad'), may hold values from -1 to 1, as said below
- coupling: float32 [8, 8], P(None, 'rad'), may hold values from 0.2 to 0.5
Outputs:
- updated: float32 [5, 8, 512, 4096], P(None, None, 'rad', 'az')
Inputs may be any that keep to these rules, and one draw needn't show every extreme that they name: `shifts`: each radius's shift; the values 0 and 4095 both occur in every draw. `block_inverse`: entries of the given block inverses.
All inputs are finite; a program needn't handle non-finite values.
Results may differ from a plain program's by a relative error of at most 0.000075.
Values sent between devices are 32-bit elements; how exact they have to be, the bound alone decides.
A program may use at most 256 MiB of HBM per device.

v0:
```python
import jax
import jax.numpy as jnp
from jax import lax
from jax.sharding import PartitionSpec as P


def shifted(block, axis, distance):
    devices = range(lax.axis_size(axis))
    route = [((i - distance) % len(devices), i) for i in devices]
    return lax.ppermute(block, axis, route)


def extended(shard, sides, width):
    for axis, dim in sides:
        peers, length = (lax.axis_size(axis), shard.shape[dim])
        up = [(i, (i + 1) % peers) for i in range(peers)]
        down = [(j, i) for i, j in up]
        last = lax.slice_in_dim(shard, length - width, length, axis=dim)
        leading = lax.slice_in_dim(shard, 0, width, axis=dim)
        before = lax.ppermute(last, axis, up)
        after = lax.ppermute(leading, axis, down)
        shard = jnp.concatenate([before, shard, after], axis=dim)
    return shard


def interface_solve(first_row, last_row, top_left, top_right, low_left, low_right, link_rates):
    band_count = link_rates.shape[1]
    crossings = band_count - 1
    nothing = jnp.zeros_like(first_row[:, 0])
    flat_zero = jnp.zeros_like(link_rates[:, :1])
    carry_base = nothing
    carry_slope = flat_zero
    records = []
    for crossing in range(crossings):
        if crossing > 0:
            back_link = (link_rates[:, crossing - 1] * low_left[:, crossing])[:, None]
        else:
            back_link = flat_zero
        self_link = (link_rates[:, crossing] * low_right[:, crossing])[:, None]
        fore_link = (link_rates[:, crossing] * top_left[:, crossing + 1])[:, None]
        if crossing + 1 < crossings:
            next_link = (link_rates[:, crossing + 1] * top_right[:, crossing + 1])[:, None]
        else:
            next_link = flat_zero
        steepness = back_link * carry_slope + self_link
        offset = last_row[:, crossing] + back_link * carry_base
        denominator = 1.0 - fore_link * steepness
        upper_base = (first_row[:, crossing + 1] + fore_link * offset) / denominator
        upper_slope = next_link / denominator
        carry_base = offset + steepness * upper_base
        carry_slope = steepness * upper_slope
        records.append((carry_base, carry_slope, upper_base, upper_slope))
    lower_values = [nothing] * crossings
    upper_values = [nothing] * crossings
    follow = nothing
    for crossing in reversed(range(crossings)):
        carry_base, carry_slope, upper_base, upper_slope = records[crossing]
        lower_values[crossing] = carry_base + carry_slope * follow
        upper_values[crossing] = upper_base + upper_slope * follow
        follow = upper_values[crossing]
    before = jnp.stack([nothing] + lower_values, axis=1)
    beyond = jnp.stack(upper_values + [nothing], axis=1)
    return (before, beyond)


def per_device(fields, velocity, shifts, block_inverse, coupling):
    shard_cells = fields.shape[3]
    shard_hops = shifts // shard_cells
    remainder = shifts - shard_hops * shard_cells
    moving = fields
    sections = (lax.axis_size("az") - 1).bit_length()
    for section in range(sections):
        arrived = shifted(moving, "az", 1 << section)
        chosen = (shard_hops >> section) % 2 == 1
        moving = jnp.where(chosen[None, None, :, None], arrived, moving)
    previous = shifted(moving, "az", 1)
    joined = jnp.concatenate([previous, moving], axis=3)
    rotated = jax.vmap(
        lambda one_row, opening: lax.dynamic_slice_in_dim(one_row, opening, shard_cells, axis=-1),
        in_axes=(2, 0),
        out_axes=2,
    )(joined, shard_cells - remainder)
    stacked = jnp.concatenate([rotated, velocity[None]], axis=0)
    padded = extended(stacked, (("az", 3),), 1)
    values = padded[:5]
    speed = padded[5:]
    outflow = (
        jnp.maximum(speed[..., :-1], 0.0) * values[..., :-1]
        + jnp.minimum(speed[..., :-1], 0.0) * values[..., 1:]
    )
    transported = values[..., 1:-1] - (outflow[..., 1:] - outflow[..., :-1])
    energy = transported[4]
    local_part = jnp.einsum("zrl,zlp->zrp", block_inverse, energy, precision=lax.Precision.HIGHEST)
    corners = jnp.stack(
        [
            block_inverse[:, 0, 0],
            block_inverse[:, 0, -1],
            block_inverse[:, -1, 0],
            block_inverse[:, -1, -1],
        ],
        axis=1,
    )[:, None, :]
    first_all, last_all, corner_all, link_all = (
        lax.all_gather(local_part[:, :1, :], "rad", axis=1, tiled=True),
        lax.all_gather(local_part[:, -1:, :], "rad", axis=1, tiled=True),
        lax.all_gather(corners, "rad", axis=1, tiled=True),
        lax.all_gather(coupling, "rad", axis=1, tiled=True),
    )
    before, beyond = interface_solve(
        first_all,
        last_all,
        corner_all[..., 0],
        corner_all[..., 1],
        corner_all[..., 2],
        corner_all[..., 3],
        link_all,
    )
    band_index = lax.axis_index("rad")
    before_own = lax.dynamic_index_in_dim(before, band_index, 1, keepdims=False)
    beyond_own = lax.dynamic_index_in_dim(beyond, band_index, 1, keepdims=False)
    link_prev = jnp.concatenate([jnp.zeros_like(link_all[:, :1]), link_all[:, :-1]], axis=1)
    prev_own = lax.dynamic_index_in_dim(link_prev, band_index, 1, keepdims=False)
    link_own = coupling[:, 0]
    diffused = (
        local_part
        + (prev_own[:, None] * block_inverse[:, :, 0])[:, :, None] * before_own[:, None, :]
        + (link_own[:, None] * block_inverse[:, :, -1])[:, :, None] * beyond_own[:, None, :]
    )
    return jnp.concatenate([transported[:4], diffused[None]], axis=0)


def solution(mesh):
    placed = (
        P(None, None, "rad", "az"),
        P(None, "rad", "az"),
        P("rad"),
        P(None, "rad", None),
        P(None, "rad"),
    )
    return jax.shard_map(
        per_device,
        mesh=mesh,
        in_specs=placed,
        out_specs=P(None, None, "rad", "az"),
        check_vma=False,
    )
```

profile of v0, /device:TPU:0, one launch (start us, length us, event | category | flops | bytes accessed | tf_op | source)
XLA Modules:
  0.0 436.5 jit_solution(17480261281971726092)
XLA Ops:
  0.0 0.7 fusion.23
  0.7 25.5 %collective-permute-done = f32[5,8,64,128]{3,2,1,0:T(8,128)S(1)} collective-permute-done((f32[5,8,64,128]{3,2,1,0:T(8,128)}, f32[5,8,64,128]{3,2,1,0:T(8,128)S(1)}, u32[]{:S(2)}, u32[]{:S(2)}) %collective-permute-start) | collective-permute-done | bytes 1310752 | tf_op jit(solution)/shard_map/ppermute | solution.py:10
  26.2 1.6 broadcast_select_fusion
  27.8 0.1 collective-permute-start.1
  27.9 38.1 %collective-permute-done.1 = f32[5,8,64,128]{3,2,1,0:T(8,128)S(1)} collective-permute-done((f32[5,8,64,128]{3,2,1,0:T(8,128)S(1)}, f32[5,8,64,128]{3,2,1,0:T(8,128)S(1)}, u32[]{:S(2)}, u32[]{:S(2)}) %collective-permute-start.1) | collective-permute-done | bytes 1310752 | tf_op jit(solution)/shard_map/ppermute | solution.py:10
  66.0 0.3 broadcast_select_fusion.1
  66.3 40.9 %collective-permute-start.2 = (f32[5,8,64,128]{3,2,1,0:T(8,128)S(1)}, f32[5,8,64,128]{3,2,1,0:T(8,128)S(1)}, u32[]{:S(2)}, u32[]{:S(2)}) collective-permute-start(f32[5,8,64,128]{3,2,1,0:T(8,128)S(1)} %broadcast_select_fusion.1), channel_id=1, source_target_pairs={{224,0},{232,8},{240,16},{248,24},{0,32},{8,40},{16,48},{24,56},{3... | collective-permute-start | bytes 3932168 | tf_op jit(solution)/shard_map/ppermute | solution.py:10
  107.1 32.1 %collective-permute-done.2 = f32[5,8,64,128]{3,2,1,0:T(8,128)S(1)} collective-permute-done((f32[5,8,64,128]{3,2,1,0:T(8,128)S(1)}, f32[5,8,64,128]{3,2,1,0:T(8,128)S(1)}, u32[]{:S(2)}, u32[]{:S(2)}) %collective-permute-start.2) | collective-permute-done | bytes 1310752 | tf_op jit(solution)/shard_map/ppermute | solution.py:10
  139.3 0.3 broadcast_select_fusion.2
  139.6 0.1 collective-permute-start.3
  139.7 40.0 %collective-permute-done.3 = f32[5,8,64,128]{3,2,1,0:T(8,128)S(1)} collective-permute-done((f32[5,8,64,128]{3,2,1,0:T(8,128)S(1)}, f32[5,8,64,128]{3,2,1,0:T(8,128)S(1)}, u32[]{:S(2)}, u32[]{:S(2)}) %collective-permute-start.3) | collective-permute-done | bytes 1310752 | tf_op jit(solution)/shard_map/ppermute | solution.py:10
  179.7 0.2 broadcast_select_fusion.3
  179.9 0.0 copy-start.35
  179.9 0.1 collective-permute-start.4
  180.0 0.6 copy-done
  180.6 0.1 fusion.46
  180.8 0.1 copy.136
  180.9 0.1 copy.137
  181.0 30.1 %all-gather.1 = f32[8,1,8]{2,1,0:T(1,128)S(1)} all-gather(f32[1,1,8]{2,1,0:T(1,128)S(1)} %bitcast.199), channel_id=1, replica_groups=mesh['az'=32,'rad'=8] {'rad'}, dimensions={0}, use_global_device_ids=true | all-gather | bytes 288 | tf_op jit(solution)/shard_map/all_gather | solution.py:107
  211.1 0.2 slice_reduce_fusion.3
  211.3 23.7 %all-gather.2 = f32[8,4,8]{2,1,0:T(4,128)S(1)} all-gather(f32[1,4,8]{2,1,0:T(4,128)S(1)} %maximum_bitcast_fusion.1), channel_id=2, replica_groups=mesh['az'=32,'rad'=8] {'rad'}, dimensions={0}, use_global_device_ids=true | all-gather | bytes 1152 | tf_op jit(solution)/shard_map/all_gather | solution.py:106
  235.0 0.6 multiply_bitcast_fusion.2
  235.7 0.5 multiply_bitcast_fusion.3
  236.2 0.5 multiply_bitcast_fusion.6
  236.7 0.2 broadcast_select_fusion.4
  237.0 0.1 collective-permute-start.5
  237.1 0.5 multiply_bitcast_fusion.8
  237.6 0.1 multiply_bitcast_fusion.1
  237.7 0.1 multiply_bitcast_fusion
  237.7 0.6 fusion.31
  238.3 0.6 fusion.37
  239.0 0.6 fusion.24
  239.6 32.1 %collective-permute-done.5 = f32[5,8,64,128]{3,2,1,0:T(8,128)S(1)} collective-permute-done((f32[5,8,64,128]{3,2,1,0:T(8,128)S(1)}, f32[5,8,64,128]{3,2,1,0:T(8,128)S(1)}, u32[]{:S(2)}, u32[]{:S(2)}) %collective-permute-start.5) | collective-permute-done | bytes 1310752 | tf_op jit(solution)/shard_map/ppermute | solution.py:10
  271.7 0.2 pad_maximum_fusion.4
  271.9 48.9 %copy.70 = f32[5,8,64,256]{1,0,2,3:T(8,128)} copy(f32[5,8,64,256]{3,2,1,0:T(8,128)S(1)} %pad_maximum_fusion.4) | data formatting | bytes 5242880 | tf_op jit(solution)/shard_map/concatenate | solution.py:77
  320.8 24.3 %gather_fusion = f32[64,5,8,128]{2,1,3,0:T(8,128)} fusion(f32[64,5,8,256]{2,1,0,3:T(8,128)} %bitcast, s32[64]{0:T(128)S(1)} %get-tuple-element.40), kind=kCustom, calls=%fused_computation | custom fusion | bytes 2622464 | tf_op jit(solution)/shard_map/vmap()/gather | solution.py:79
  345.1 13.7 %copy.71 = f32[64,5,8,128]{3,0,2,1:T(8,128)S(1)} copy(f32[64,5,8,128]{2,1,3,0:T(8,128)} %gather_fusion) | data formatting | bytes 2621440 | tf_op jit(solution)/shard_map/vmap()/gather | solution.py:79
  358.9 1.8 slice_maximum_fusion
  360.6 1.9 copy.72
  362.6 0.2 collective-permute-start.6
  362.8 0.6 constant_dynamic-update-slice_fusion.7
  363.4 0.5 copy.74
  363.9 6.0 %collective-permute-start.7 = (f32[6,8,64,1]{2,1,3,0:T(8,128)S(1)}, f32[6,8,64,1]{2,1,3,0:T(8,128)S(1)}, u32[]{:S(2)}, u32[]{:S(2)}) collective-permute-start(f32[6,8,64,1]{2,1,3,0:T(8,128)S(1)} %copy.74), channel_id=1, source_target_pairs={{8,0},{16,8},{24,16},{32,24},{40,32},{48,40},{56,48},{64,56},{72,6... | collective-permute-start | bytes 36872 | tf_op jit(solution)/shard_map/ppermute | solution.py:21
  369.9 0.3 collective-permute-done.6
  370.3 0.5 copy.73
  370.8 1.0 maximum_bitcast_fusion
  371.8 0.8 minimum_bitcast_fusion
  372.7 1.7 copy.75
  374.4 2.3 fusion.1
  376.7 0.5 fusion.3
  377.2 0.4 convolution_bitcast_fusion
  377.9 0.1 slice.318
  378.0 28.1 %all_gather.13 = f32[8,8,128]{2,0,1:T(8,128)S(1)} all-gather(f32[8,1,128]{2,0,1:T(8,128)S(1)} %bitcast.178), channel_id=1, replica_groups=mesh['az'=32,'rad'=8] {'rad'}, dimensions={1}, use_global_device_ids=true | all-gather | bytes 36864 | tf_op jit(solution)/shard_map/all_gather | solution.py:105
  406.1 28.0 %all_gather.15 = f32[8,8,128]{2,0,1:T(8,128)S(1)} all-gather(f32[8,1,128]{2,0,1:T(8,128)S(1)} %bitcast.177), channel_id=1, replica_groups=mesh['az'=32,'rad'=8] {'rad'}, dimensions={1}, use_global_device_ids=true | all-gather | bytes 36864 | tf_op jit(solution)/shard_map/all_gather | solution.py:104
  434.4 0.2 constant_dynamic-update-slice_fusion.6
  434.6 0.1 constant_dynamic-update-slice_fusion.15
  434.6 0.1 constant_dynamic-update-slice_fusion.5
  434.7 0.1 constant_dynamic-update-slice_fusion.4
  434.8 0.1 constant_dynamic-update-slice_fusion.3
  434.9 0.1 constant_dynamic-update-slice_fusion.2
  435.0 0.1 constant_dynamic-update-slice_fusion.1
  435.1 0.1 constant_dynamic-update-slice_fusion
  435.2 0.2 add_bitcast_fusion
  435.4 1.1 pad_maximum_fusion.6
  (96 shorter events, 0.3 us)
Async XLA Ops:
  0.0 26.2 %collective-permute-start = (f32[5,8,64,128]{3,2,1,0:T(8,128)}, f32[5,8,64,128]{3,2,1,0:T(8,128)S(1)}, u32[]{:S(2)}, u32[]{:S(2)}) collective-permute-start(f32[5,8,64,128]{3,2,1,0:T(8,128)} %param.5), channel_id=1, source_target_pairs={{248,0},{0,8},{8,16},{16,24},{24,32},{32,40},{40,48},{48,56},{56,6... | collective-permute-start | bytes 3932168 | tf_op jit(solution)/shard_map/ppermute | solution.py:10
  27.8 38.1 %collective-permute-start.1 = (f32[5,8,64,128]{3,2,1,0:T(8,128)S(1)}, f32[5,8,64,128]{3,2,1,0:T(8,128)S(1)}, u32[]{:S(2)}, u32[]{:S(2)}) collective-permute-start(f32[5,8,64,128]{3,2,1,0:T(8,128)S(1)} %broadcast_select_fusion), channel_id=1, source_target_pairs={{240,0},{248,8},{0,16},{8,24},{16,32},{24,40},{32,48},{40,56},{48,... | collective-permute-start | bytes 3932168 | tf_op jit(solution)/shard_map/ppermute | solution.py:10
  66.3 73.0 %collective-permute-start.2 = (f32[5,8,64,128]{3,2,1,0:T(8,128)S(1)}, f32[5,8,64,128]{3,2,1,0:T(8,128)S(1)}, u32[]{:S(2)}, u32[]{:S(2)}) collective-permute-start(f32[5,8,64,128]{3,2,1,0:T(8,128)S(1)} %broadcast_select_fusion.1), channel_id=1, source_target_pairs={{224,0},{232,8},{240,16},{248,24},{0,32},{8,40},{16,48},{24,56},{3... | collective-permute-start | bytes 3932168 | tf_op jit(solution)/shard_map/ppermute | solution.py:10
  139.6 40.1 %collective-permute-start.3 = (f32[5,8,64,128]{3,2,1,0:T(8,128)S(1)}, f32[5,8,64,128]{3,2,1,0:T(8,128)S(1)}, u32[]{:S(2)}, u32[]{:S(2)}) collective-permute-start(f32[5,8,64,128]{3,2,1,0:T(8,128)S(1)} %broadcast_select_fusion.2), channel_id=1, source_target_pairs={{192,0},{200,8},{208,16},{216,24},{224,32},{232,40},{240,48},{248,... | collective-permute-start | bytes 3932168 | tf_op jit(solution)/shard_map/ppermute | solution.py:10
  179.7 1.0 copy-start
  179.9 1.1 copy-start.35
  179.9 56.8 %collective-permute-start.4 = (f32[5,8,64,128]{3,2,1,0:T(8,128)S(1)}, f32[5,8,64,128]{3,2,1,0:T(8,128)S(1)}, u32[]{:S(2)}, u32[]{:S(2)}) collective-permute-start(f32[5,8,64,128]{3,2,1,0:T(8,128)S(1)} %broadcast_select_fusion.3), channel_id=1, source_target_pairs={{128,0},{136,8},{144,16},{152,24},{160,32},{168,40},{176,48},{184,... | collective-permute-start | bytes 3932168 | tf_op jit(solution)/shard_map/ppermute | solution.py:10
  235.6 1.4 copy-start.2
  235.6 1.4 copy-start.14
  235.6 1.4 copy-start.16
  235.6 1.5 copy-start.22
  235.6 2.7 copy-start.20
  235.7 3.3 copy-start.4
  235.7 3.3 copy-start.6
  235.7 3.3 copy-start.18
  237.0 34.7 %collective-permute-start.5 = (f32[5,8,64,128]{3,2,1,0:T(8,128)S(1)}, f32[5,8,64,128]{3,2,1,0:T(8,128)S(1)}, u32[]{:S(2)}, u32[]{:S(2)}) collective-permute-start(f32[5,8,64,128]{3,2,1,0:T(8,128)S(1)} %broadcast_select_fusion.4), channel_id=1, source_target_pairs={{248,0},{0,8},{8,16},{16,24},{24,32},{32,40},{40,48},{48,56},{56,6... | collective-permute-start | bytes 3932168 | tf_op jit(solution)/shard_map/ppermute | solution.py:10
  345.1 13.8 %copy-start.1 = (f32[8,64,128]{2,1,0:T(8,128)S(1)}, f32[8,64,128]{2,1,0:T(8,128)}, u32[]{:S(2)}) copy-start(f32[8,64,128]{2,1,0:T(8,128)} %param.6) | copy-start | bytes 786436
  362.6 7.7 %collective-permute-start.6 = (f32[6,8,64,1]{2,1,3,0:T(8,128)S(1)}, f32[6,8,64,1]{2,1,3,0:T(8,128)S(1)}, u32[]{:S(2)}, u32[]{:S(2)}) collective-permute-start(f32[6,8,64,1]{2,1,3,0:T(8,128)S(1)} %copy.72), channel_id=1, source_target_pairs={{0,8},{8,16},{16,24},{24,32},{32,40},{40,48},{48,56},{56,64},{64,7... | collective-permute-start | bytes 36872 | tf_op jit(solution)/shard_map/ppermute | solution.py:20
  363.9 8.7 %collective-permute-start.7 = (f32[6,8,64,1]{2,1,3,0:T(8,128)S(1)}, f32[6,8,64,1]{2,1,3,0:T(8,128)S(1)}, u32[]{:S(2)}, u32[]{:S(2)}) collective-permute-start(f32[6,8,64,1]{2,1,3,0:T(8,128)S(1)} %copy.74), channel_id=1, source_target_pairs={{8,0},{16,8},{24,16},{32,24},{40,32},{48,40},{56,48},{64,56},{72,6... | collective-permute-start | bytes 36872 | tf_op jit(solution)/shard_map/ppermute | solution.py:21
  377.6 56.6 %copy-start.3 = (f32[8,1]{0,1:T(1,128)S(1)}, f32[8,1]{0,1:T(1,128)}, u32[]{:S(2)}) copy-start(f32[8,1]{0,1:T(1,128)} %copy-done.2) | copy-start | bytes 100
  377.6 56.5 %copy-start.5 = (f32[8,1]{0,1:T(1,128)S(1)}, f32[8,1]{0,1:T(1,128)}, u32[]{:S(2)}) copy-start(f32[8,1]{0,1:T(1,128)} %copy-done.4) | copy-start | bytes 100
  377.6 56.5 %copy-start.7 = (f32[8,1]{0,1:T(1,128)S(1)}, f32[8,1]{0,1:T(1,128)}, u32[]{:S(2)}) copy-start(f32[8,1]{0,1:T(1,128)} %copy-done.6) | copy-start | bytes 100
  377.6 56.5 %copy-start.8 = (f32[8]{0:T(128)S(1)}, f32[8]{0:T(128)}, u32[]{:S(2)}) copy-start(f32[8]{0:T(128)} %get-tuple-element.53) | copy-start | bytes 100
  377.6 56.5 %copy-start.9 = (f32[8]{0:T(128)S(1)}, f32[8]{0:T(128)}, u32[]{:S(2)}) copy-start(f32[8]{0:T(128)} %get-tuple-element.63) | copy-start | bytes 100
  377.7 56.5 %copy-start.10 = (f32[8]{0:T(128)S(1)}, f32[8]{0:T(128)}, u32[]{:S(2)}) copy-start(f32[8]{0:T(128)} %get-tuple-element.55) | copy-start | bytes 100
  377.7 56.5 %copy-start.11 = (f32[8]{0:T(128)S(1)}, f32[8]{0:T(128)}, u32[]{:S(2)}) copy-start(f32[8]{0:T(128)} %get-tuple-element.64) | copy-start | bytes 100
  377.7 56.5 %copy-start.12 = (f32[8]{0:T(128)S(1)}, f32[8]{0:T(128)}, u32[]{:S(2)}) copy-start(f32[8]{0:T(128)} %get-tuple-element.57) | copy-start | bytes 100
  377.7 56.5 %copy-start.13 = (f32[8]{0:T(128)S(1)}, f32[8]{0:T(128)}, u32[]{:S(2)}) copy-start(f32[8]{0:T(128)} %get-tuple-element.65) | copy-start | bytes 100
  377.7 56.5 %copy-start.15 = (f32[8,1]{0,1:T(1,128)S(1)}, f32[8,1]{0,1:T(1,128)}, u32[]{:S(2)}) copy-start(f32[8,1]{0,1:T(1,128)} %copy-done.14) | copy-start | bytes 100
  377.7 56.5 %copy-start.17 = (f32[8,1]{0,1:T(1,128)S(1)}, f32[8,1]{0,1:T(1,128)}, u32[]{:S(2)}) copy-start(f32[8,1]{0,1:T(1,128)} %copy-done.16) | copy-start | bytes 100
  377.7 56.5 %copy-start.23 = (f32[8,1]{0,1:T(1,128)S(1)}, f32[8,1]{0,1:T(1,128)}, u32[]{:S(2)}) copy-start(f32[8,1]{0,1:T(1,128)} %copy-done.22) | copy-start | bytes 100
  377.7 56.5 %copy-start.24 = (f32[8]{0:T(128)S(1)}, f32[8]{0:T(128)}, u32[]{:S(2)}) copy-start(f32[8]{0:T(128)} %get-tuple-element.66) | copy-start | bytes 100
  377.7 56.5 %copy-start.25 = (f32[8]{0:T(128)S(1)}, f32[8]{0:T(128)}, u32[]{:S(2)}) copy-start(f32[8]{0:T(128)} %get-tuple-element.67) | copy-start | bytes 100
  377.7 56.5 %copy-start.26 = (f32[8]{0:T(128)S(1)}, f32[8]{0:T(128)}, u32[]{:S(2)}) copy-start(f32[8]{0:T(128)} %get-tuple-element.68) | copy-start | bytes 100
  377.8 56.5 %copy-start.27 = (f32[8]{0:T(128)S(1)}, f32[8]{0:T(128)}, u32[]{:S(2)}) copy-start(f32[8]{0:T(128)} %get-tuple-element.69) | copy-start | bytes 100
  377.8 56.5 %copy-start.28 = (f32[8]{0:T(128)S(1)}, f32[8]{0:T(128)}, u32[]{:S(2)}) copy-start(f32[8]{0:T(128)} %get-tuple-element.70) | copy-start | bytes 100
  377.8 56.5 %copy-start.29 = (f32[8]{0:T(128)S(1)}, f32[8]{0:T(128)}, u32[]{:S(2)}) copy-start(f32[8]{0:T(128)} %get-tuple-element.71) | copy-start | bytes 100
  377.8 56.5 %copy-start.30 = (f32[8]{0:T(128)S(1)}, f32[8]{0:T(128)}, u32[]{:S(2)}) copy-start(f32[8]{0:T(128)} %get-tuple-element.52) | copy-start | bytes 100
  377.8 56.5 %copy-start.31 = (f32[8]{0:T(128)S(1)}, f32[8]{0:T(128)}, u32[]{:S(2)}) copy-start(f32[8]{0:T(128)} %get-tuple-element.56) | copy-start | bytes 100
  377.8 56.5 %copy-start.32 = (f32[8]{0:T(128)S(1)}, f32[8]{0:T(128)}, u32[]{:S(2)}) copy-start(f32[8]{0:T(128)} %get-tuple-element.58) | copy-start | bytes 100
  377.8 56.5 %copy-start.33 = (f32[8]{0:T(128)S(1)}, f32[8]{0:T(128)}, u32[]{:S(2)}) copy-start(f32[8]{0:T(128)} %get-tuple-element.59) | copy-start | bytes 100
  377.8 56.5 %copy-start.34 = (f32[8]{0:T(128)S(1)}, f32[8]{0:T(128)}, u32[]{:S(2)}) copy-start(f32[8]{0:T(128)} %get-tuple-element.83) | copy-start | bytes 100
  377.8 56.5 %copy-start.38 = (f32[8,8,128]{2,0,1:T(8,128)S(1)}, f32[8,8,128]{2,0,1:T(8,128)}, u32[]{:S(2)}) copy-start(f32[8,8,128]{2,0,1:T(8,128)} %constant_dynamic-update-slice_fusion.7) | copy-start | bytes 98308
  377.8 56.7 %copy-start.19 = (f32[8,1]{0,1:T(1,128)S(1)}, f32[8,1]{0,1:T(1,128)}, u32[]{:S(2)}) copy-start(f32[8,1]{0,1:T(1,128)} %copy-done.18) | copy-start | bytes 100
  377.9 56.8 %copy-start.42 = (f32[8]{0:T(128)S(1)}, f32[8]{0:T(128)}, u32[]{:S(2)}) copy-start(f32[8]{0:T(128)} %multiply_bitcast_fusion.8) | copy-start | bytes 100
  377.9 56.9 %copy-start.40 = (f32[8]{0:T(128)S(1)}, f32[8]{0:T(128)}, u32[]{:S(2)}) copy-start(f32[8]{0:T(128)} %get-tuple-element.92) | copy-start | bytes 100
  377.9 56.9 %copy-start.39 = (f32[8]{0:T(128)S(1)}, f32[8]{0:T(128)}, u32[]{:S(2)}) copy-start(f32[8]{0:T(128)} %get-tuple-element.91) | copy-start | bytes 100
  377.9 57.0 %copy-start.37 = (f32[8]{0:T(128)S(1)}, f32[8]{0:T(128)}, u32[]{:S(2)}) copy-start(f32[8]{0:T(128)} %get-tuple-element.82) | copy-start | bytes 100
  377.9 57.1 %copy-start.36 = (f32[8]{0:T(128)S(1)}, f32[8]{0:T(128)}, u32[]{:S(2)}) copy-start(f32[8]{0:T(128)} %get-tuple-element.90) | copy-start | bytes 100
  377.9 57.1 %copy-start.21 = (f32[8,1]{0,1:T(1,128)S(1)}, f32[8,1]{0,1:T(1,128)}, u32[]{:S(2)}) copy-start(f32[8,1]{0,1:T(1,128)} %copy-done.20) | copy-start | bytes 100
  377.9 57.1 %copy-start.41 = (f32[8]{0:T(128)S(1)}, f32[8]{0:T(128)}, u32[]{:S(2)}) copy-start(f32[8]{0:T(128)} %get-tuple-element.9) | copy-start | bytes 100
where the time goes:
time: 437 us
  waiting for transfers between devices  168 us (38%)
  blocking collectives  110 us (25%)
  local copies, waits for them, and re-layouts  93.7 us (21%)
  starting transfers between devices  47.4 us (11%)
  other arithmetic  16.2 us (4%)
    ppermute x6, waiting for transfers between devices, shifted(): return lax.ppermute(block, axis, route)  168 us
    concatenate x1, local copies, waits for them, and re-layouts, per_device(): joined = jnp.concatenate([previous, moving], axis=3)  48.9 us
    ppermute x6, starting transfers between devices, shifted(): return lax.ppermute(block, axis, route)  41.2 us
    gather x2, local copies, waits for them, and re-layouts, per_device(): lax.dynamic_slice_in_dim(one_row, opening, shard_cells, axis=-1)  38 us
    all_gather x1, blocking collectives, per_device(): lax.all_gather(coupling, 'rad', axis=1, tiled=True)  30.1 us
    all_gather x1, blocking collectives, per_device(): lax.all_gather(local_part[:, -1:, :], 'rad', axis=1, tiled=True)  28.1 us
    all_gather x1, blocking collectives, per_device(): lax.all_gather(local_part[:, :1, :], 'rad', axis=1, tiled=True)  28 us
    all_gather x1, blocking collectives, per_device(): lax.all_gather(corners, 'rad', axis=1, tiled=True)  23.7 us
  transfers between devices with their start and end apart: 8, of which 6 were waited for; matrix products, arithmetic and copies ran while one was open for 2% of the time, Pallas kernels for 0%

commit v1 on v0

--- a/solution.py
+++ b/solution.py
@@ -103,7 +103,15 @@
     first_all, last_all, corner_all, link_all = (
         lax.all_gather(local_part[:, :1, :], "rad", axis=1, tiled=True),
         lax.all_gather(local_part[:, -1:, :], "rad", axis=1, tiled=True),
-        lax.all_gather(corners, "rad", axis=1, tiled=True),
+        jnp.concatenate(
+            lax.all_to_all(
+                jnp.stack([corners for _ in range(lax.axis_size("rad"))], axis=0),
+                axis_name="rad",
+                split_axis=0,
+                concat_axis=0,
+            ),
+            axis=1,
+        ),
         lax.all_gather(coupling, "rad", axis=1, tiled=True),
     )
     before, beyond = interface_solve(

time: 437 us -> 420 us (0.961)
  blocking collectives: 110 us -> 75.4 us
  starting transfers between devices: 47.4 us -> 74.3 us
  waiting for transfers between devices: 168 us -> 151 us
  local copies, waits for them, and re-layouts: 93.7 us -> 99.6 us
    all_to_all x0 -> x1, starting transfers between devices: none -> 26.8 us  [per_device(): lax.all_to_all(jnp.stack([corners for _ in range(lax.axis_size('rad'))],...]
    all_gather x1 -> x0, blocking collectives: 23.7 us -> none  [per_device(): lax.all_gather(corners, 'rad', axis=1, tiled=True)]
    ppermute x6, waiting for transfers between devices: 168 us -> 150 us  [shifted(): return lax.ppermute(block, axis, route)]
    all_gather x1, blocking collectives: 30.1 us -> 19.1 us  [per_device(): lax.all_gather(coupling, 'rad', axis=1, tiled=True)]
    unnamed x90 -> x118, local copies, waits for them, and re-layouts: 1.63 us -> 6.09 us
  transfers between devices with their start and end apart: 8 -> 9, of which waited for: 6 -> 6; matrix products, arithmetic and copies ran while one was open for 2% -> 4% of each run, Pallas kernels for 0% -> 0%
where the time goes in v1:
time: 420 us
  waiting for transfers between devices  151 us (36%)
  local copies, waits for them, and re-layouts  99.6 us (24%)
  blocking collectives  75.4 us (18%)
  starting transfers between devices  74.3 us (18%)
  other arithmetic  19 us (5%)
    ppermute x6, waiting for transfers between devices, shifted(): return lax.ppermute(block, axis, route)  150 us
    concatenate x1, local copies, waits for them, and re-layouts, per_device(): joined = jnp.concatenate([previous, moving], axis=3)  48.9 us
    ppermute x6, starting transfers between devices, shifted(): return lax.ppermute(block, axis, route)  41.2 us
    gather x2, local copies, waits for them, and re-layouts, per_device(): lax.dynamic_slice_in_dim(one_row, opening, shard_cells, axis=-1)  38 us
    all_gather x1, blocking collectives, per_device(): lax.all_gather(local_part[:, -1:, :], 'rad', axis=1, tiled=True)  28.2 us
    all_gather x1, blocking collectives, per_device(): lax.all_gather(local_part[:, :1, :], 'rad', axis=1, tiled=True)  28 us
    all_to_all x1, starting transfers between devices, per_device(): lax.all_to_all(jnp.stack([corners for _ in range(lax.axis_size('rad'))],...  26.8 us
    all_gather x1, blocking collectives, per_device(): lax.all_gather(coupling, 'rad', axis=1, tiled=True)  19.1 us
  transfers between devices with their start and end apart: 9, of which 6 were waited for; matrix products, arithmetic and copies ran while one was open for 4% of the time, Pallas kernels for 0%

profile of v1, /device:TPU:0, one launch (start us, length us, event | category | flops | bytes accessed | tf_op | source)
XLA Modules:
  0.0 419.8 jit_solution(15379997158447839926)
XLA Ops:
  0.0 0.7 fusion.23
  0.7 25.5 %collective-permute-done = f32[5,8,64,128]{3,2,1,0:T(8,128)S(1)} collective-permute-done((f32[5,8,64,128]{3,2,1,0:T(8,128)}, f32[5,8,64,128]{3,2,1,0:T(8,128)S(1)}, u32[]{:S(2)}, u32[]{:S(2)}) %collective-permute-start) | collective-permute-done | bytes 1310752 | tf_op jit(solution)/shard_map/ppermute | solution.py:10
  26.2 1.6 broadcast_select_fusion
  27.8 0.1 collective-permute-start.1
  27.9 38.1 %collective-permute-done.1 = f32[5,8,64,128]{3,2,1,0:T(8,128)S(1)} collective-permute-done((f32[5,8,64,128]{3,2,1,0:T(8,128)S(1)}, f32[5,8,64,128]{3,2,1,0:T(8,128)S(1)}, u32[]{:S(2)}, u32[]{:S(2)}) %collective-permute-start.1) | collective-permute-done | bytes 1310752 | tf_op jit(solution)/shard_map/ppermute | solution.py:10
  66.0 0.3 broadcast_select_fusion.1
  66.3 40.9 %collective-permute-start.2 = (f32[5,8,64,128]{3,2,1,0:T(8,128)S(1)}, f32[5,8,64,128]{3,2,1,0:T(8,128)S(1)}, u32[]{:S(2)}, u32[]{:S(2)}) collective-permute-start(f32[5,8,64,128]{3,2,1,0:T(8,128)S(1)} %broadcast_select_fusion.1), channel_id=1, source_target_pairs={{224,0},{232,8},{240,16},{248,24},{0,32},{8,40},{16,48},{24,56},{3... | collective-permute-start | bytes 3932168 | tf_op jit(solution)/shard_map/ppermute | solution.py:10
  107.1 32.1 %collective-permute-done.2 = f32[5,8,64,128]{3,2,1,0:T(8,128)S(1)} collective-permute-done((f32[5,8,64,128]{3,2,1,0:T(8,128)S(1)}, f32[5,8,64,128]{3,2,1,0:T(8,128)S(1)}, u32[]{:S(2)}, u32[]{:S(2)}) %collective-permute-start.2) | collective-permute-done | bytes 1310752 | tf_op jit(solution)/shard_map/ppermute | solution.py:10
  139.3 0.2 broadcast_select_fusion.2
  139.5 0.1 collective-permute-start.3
  139.6 0.6 copy-done.1
  140.2 0.2 slice_reduce_fusion.3
  140.5 0.6 stack.9
  141.1 26.8 %all-to-all-start = ((f32[8,8,1,4]{1,3,2,0:T(4,128)}), f32[8,8,1,4]{1,3,2,0:T(4,128)S(1)}, u32[]{:S(2)}, u32[]{:S(2)}) async-start(f32[8,8,1,4]{1,3,2,0:T(4,128)} %stack.9), calls=%async_computation | async-start | bytes 32768 | tf_op jit(solution)/shard_map/all_to_all | solution.py:107
  167.9 0.8 fusion.29
  168.6 1.1 copy.103
  169.7 0.1 copy.130
  169.9 19.1 %all-gather = f32[8,1,8]{2,1,0:T(1,128)S(1)} all-gather(f32[1,1,8]{2,1,0:T(1,128)S(1)} %bitcast.160), channel_id=1, replica_groups=mesh['az'=32,'rad'=8] {'rad'}, dimensions={0}, use_global_device_ids=true | all-gather | bytes 288 | tf_op jit(solution)/shard_map/all_gather | solution.py:115
  189.1 0.6 constant_dynamic-update-slice_fusion.7
  189.8 1.1 copy-done.3
  190.9 1.6 broadcast_select_fusion.3
  192.4 0.1 collective-permute-start.4
  192.6 0.1 copy.105
  192.7 0.1 copy.107
  192.9 0.1 copy.119
  193.1 0.1 copy.127
  193.8 0.1 copy.108
  194.8 0.7 multiply_bitcast_fusion.2
  195.5 0.6 multiply_bitcast_fusion.19
  196.1 0.5 multiply_bitcast_fusion.15
  196.6 22.2 %collective-permute-done.4 = f32[5,8,64,128]{3,2,1,0:T(8,128)S(1)} collective-permute-done((f32[5,8,64,128]{3,2,1,0:T(8,128)S(1)}, f32[5,8,64,128]{3,2,1,0:T(8,128)S(1)}, u32[]{:S(2)}, u32[]{:S(2)}) %collective-permute-start.4) | collective-permute-done | bytes 1310752 | tf_op jit(solution)/shard_map/ppermute | solution.py:10
  218.8 0.2 broadcast_select_fusion.4
  219.1 0.1 collective-permute-start.5
  219.2 0.5 multiply_bitcast_fusion.12
  219.7 0.5 multiply_bitcast_fusion.9
  220.2 0.5 multiply_bitcast_fusion.6
  220.7 0.5 multiply_bitcast_fusion.4
  221.2 0.6 multiply_bitcast_fusion.13
  221.8 0.6 fusion.24
  222.4 32.2 %collective-permute-done.5 = f32[5,8,64,128]{3,2,1,0:T(8,128)S(1)} collective-permute-done((f32[5,8,64,128]{3,2,1,0:T(8,128)S(1)}, f32[5,8,64,128]{3,2,1,0:T(8,128)S(1)}, u32[]{:S(2)}, u32[]{:S(2)}) %collective-permute-start.5) | collective-permute-done | bytes 1310752 | tf_op jit(solution)/shard_map/ppermute | solution.py:10
  254.6 0.2 pad_maximum_fusion.4
  254.8 48.9 %copy.66 = f32[5,8,64,256]{1,0,2,3:T(8,128)} copy(f32[5,8,64,256]{3,2,1,0:T(8,128)S(1)} %pad_maximum_fusion.4) | data formatting | bytes 5242880 | tf_op jit(solution)/shard_map/concatenate | solution.py:77
  303.7 24.3 %gather_fusion = f32[64,5,8,128]{2,1,3,0:T(8,128)} fusion(f32[64,5,8,256]{2,1,0,3:T(8,128)} %bitcast, s32[64]{0:T(128)S(1)} %get-tuple-element.47), kind=kCustom, calls=%fused_computation | custom fusion | bytes 2622464 | tf_op jit(solution)/shard_map/vmap()/gather | solution.py:79
  328.0 13.7 %copy.67 = f32[64,5,8,128]{3,0,2,1:T(8,128)S(1)} copy(f32[64,5,8,128]{2,1,3,0:T(8,128)} %gather_fusion) | data formatting | bytes 2621440 | tf_op jit(solution)/shard_map/vmap()/gather | solution.py:79
  341.7 1.8 slice_maximum_fusion
  343.5 1.9 copy.68
  345.5 0.2 collective-permute-start.6
  345.7 0.5 multiply_bitcast_fusion.3
  346.2 0.5 copy.70
  346.7 6.0 %collective-permute-start.7 = (f32[6,8,64,1]{2,1,3,0:T(8,128)S(1)}, f32[6,8,64,1]{2,1,3,0:T(8,128)S(1)}, u32[]{:S(2)}, u32[]{:S(2)}) collective-permute-start(f32[6,8,64,1]{2,1,3,0:T(8,128)S(1)} %copy.70), channel_id=1, source_target_pairs={{8,0},{16,8},{24,16},{32,24},{40,32},{48,40},{56,48},{64,56},{72,6... | collective-permute-start | bytes 36872 | tf_op jit(solution)/shard_map/ppermute | solution.py:21
  352.7 0.5 collective-permute-done.6
  353.2 0.5 copy.69
  353.7 1.0 maximum_bitcast_fusion
  354.7 0.9 minimum_bitcast_fusion
  355.6 1.7 copy.71
  357.3 2.3 fusion.1
  359.7 0.5 fusion.3
  360.1 0.4 convolution_bitcast_fusion
  360.8 0.3 copy-done
  361.2 28.2 %all_gather.10 = f32[8,8,128]{2,0,1:T(8,128)S(1)} all-gather(f32[8,1,128]{2,0,1:T(8,128)S(1)} %bitcast.129), channel_id=1, replica_groups=mesh['az'=32,'rad'=8] {'rad'}, dimensions={1}, use_global_device_ids=true | all-gather | bytes 36864 | tf_op jit(solution)/shard_map/all_gather | solution.py:105
  389.4 28.0 %all_gather.11 = f32[8,8,128]{2,0,1:T(8,128)S(1)} all-gather(f32[8,1,128]{2,0,1:T(8,128)S(1)} %bitcast.128), channel_id=1, replica_groups=mesh['az'=32,'rad'=8] {'rad'}, dimensions={1}, use_global_device_ids=true | all-gather | bytes 36864 | tf_op jit(solution)/shard_map/all_gather | solution.py:104
  417.7 0.2 constant_dynamic-update-slice_fusion.6
  418.5 0.2 add_bitcast_fusion
  418.7 1.1 pad_maximum_fusion.6
  (133 shorter events, 2.9 us)
Async XLA Ops:
  0.0 26.2 %collective-permute-start = (f32[5,8,64,128]{3,2,1,0:T(8,128)}, f32[5,8,64,128]{3,2,1,0:T(8,128)S(1)}, u32[]{:S(2)}, u32[]{:S(2)}) collective-permute-start(f32[5,8,64,128]{3,2,1,0:T(8,128)} %param.5), channel_id=1, source_target_pairs={{248,0},{0,8},{8,16},{16,24},{24,32},{32,40},{40,48},{48,56},{56,6... | collective-permute-start | bytes 3932168 | tf_op jit(solution)/shard_map/ppermute | solution.py:10
  27.8 38.1 %collective-permute-start.1 = (f32[5,8,64,128]{3,2,1,0:T(8,128)S(1)}, f32[5,8,64,128]{3,2,1,0:T(8,128)S(1)}, u32[]{:S(2)}, u32[]{:S(2)}) collective-permute-start(f32[5,8,64,128]{3,2,1,0:T(8,128)S(1)} %broadcast_select_fusion), channel_id=1, source_target_pairs={{240,0},{248,8},{0,16},{8,24},{16,32},{24,40},{32,48},{40,56},{48,... | collective-permute-start | bytes 3932168 | tf_op jit(solution)/shard_map/ppermute | solution.py:10
  66.3 73.0 %collective-permute-start.2 = (f32[5,8,64,128]{3,2,1,0:T(8,128)S(1)}, f32[5,8,64,128]{3,2,1,0:T(8,128)S(1)}, u32[]{:S(2)}, u32[]{:S(2)}) collective-permute-start(f32[5,8,64,128]{3,2,1,0:T(8,128)S(1)} %broadcast_select_fusion.1), channel_id=1, source_target_pairs={{224,0},{232,8},{240,16},{248,24},{0,32},{8,40},{16,48},{24,56},{3... | collective-permute-start | bytes 3932168 | tf_op jit(solution)/shard_map/ppermute | solution.py:10
  139.3 1.0 copy-start.1
  139.5 30.3 %copy-start.36 = (f32[8,1]{0,1:T(1,128)S(1)}, f32[8,1]{0,1:T(1,128)}, u32[]{:S(2)}) copy-start(f32[8,1]{0,1:T(1,128)} %param.9) | copy-start | bytes 100
  139.5 50.3 %collective-permute-start.3 = (f32[5,8,64,128]{3,2,1,0:T(8,128)S(1)}, f32[5,8,64,128]{3,2,1,0:T(8,128)S(1)}, u32[]{:S(2)}, u32[]{:S(2)}) collective-permute-start(f32[5,8,64,128]{3,2,1,0:T(8,128)S(1)} %broadcast_select_fusion.2), channel_id=1, source_target_pairs={{192,0},{200,8},{208,16},{216,24},{224,32},{232,40},{240,48},{248,... | collective-permute-start | bytes 3932168 | tf_op jit(solution)/shard_map/ppermute | solution.py:10
  141.1 48.7 %all-to-all-start = ((f32[8,8,1,4]{1,3,2,0:T(4,128)}), f32[8,8,1,4]{1,3,2,0:T(4,128)S(1)}, u32[]{:S(2)}, u32[]{:S(2)}) async-start(f32[8,8,1,4]{1,3,2,0:T(4,128)} %stack.9), calls=%async_computation | async-start | bytes 32768 | tf_op jit(solution)/shard_map/all_to_all | solution.py:107
  189.8 1.1 copy-start.3
  192.4 26.4 %collective-permute-start.4 = (f32[5,8,64,128]{3,2,1,0:T(8,128)S(1)}, f32[5,8,64,128]{3,2,1,0:T(8,128)S(1)}, u32[]{:S(2)}, u32[]{:S(2)}) collective-permute-start(f32[5,8,64,128]{3,2,1,0:T(8,128)S(1)} %broadcast_select_fusion.3), channel_id=1, source_target_pairs={{128,0},{136,8},{144,16},{152,24},{160,32},{168,40},{176,48},{184,... | collective-permute-start | bytes 3932168 | tf_op jit(solution)/shard_map/ppermute | solution.py:10
  195.5 23.6 %copy-start.18 = (f32[8,1]{0,1:T(1,128)}, f32[8,1]{0,1:T(1,128)S(1)}, u32[]{:S(2)}) copy-start(f32[8,1]{0,1:T(1,128)S(1)} %get-tuple-element.25) | copy-start | bytes 100
  195.5 23.6 %copy-start.21 = (f32[8,1]{0,1:T(1,128)}, f32[8,1]{0,1:T(1,128)S(1)}, u32[]{:S(2)}) copy-start(f32[8,1]{0,1:T(1,128)S(1)} %get-tuple-element.30) | copy-start | bytes 100
  195.5 23.6 %copy-start.23 = (f32[8,1]{0,1:T(1,128)}, f32[8,1]{0,1:T(1,128)S(1)}, u32[]{:S(2)}) copy-start(f32[8,1]{0,1:T(1,128)S(1)} %get-tuple-element.28) | copy-start | bytes 100
  195.5 23.7 %copy-start.16 = (f32[8,1]{0,1:T(1,128)}, f32[8,1]{0,1:T(1,128)S(1)}, u32[]{:S(2)}) copy-start(f32[8,1]{0,1:T(1,128)S(1)} %get-tuple-element.22) | copy-start | bytes 100
  195.5 24.2 %copy-start.14 = (f32[8,1]{0,1:T(1,128)}, f32[8,1]{0,1:T(1,128)S(1)}, u32[]{:S(2)}) copy-start(f32[8,1]{0,1:T(1,128)S(1)} %get-tuple-element.19) | copy-start | bytes 100
  195.5 24.7 %copy-start.12 = (f32[8,1]{0,1:T(1,128)}, f32[8,1]{0,1:T(1,128)S(1)}, u32[]{:S(2)}) copy-start(f32[8,1]{0,1:T(1,128)S(1)} %get-tuple-element.16) | copy-start | bytes 100
  195.5 25.2 %copy-start.10 = (f32[8,1]{0,1:T(1,128)}, f32[8,1]{0,1:T(1,128)S(1)}, u32[]{:S(2)}) copy-start(f32[8,1]{0,1:T(1,128)S(1)} %get-tuple-element.13) | copy-start | bytes 100
  219.1 35.5 %collective-permute-start.5 = (f32[5,8,64,128]{3,2,1,0:T(8,128)S(1)}, f32[5,8,64,128]{3,2,1,0:T(8,128)S(1)}, u32[]{:S(2)}, u32[]{:S(2)}) collective-permute-start(f32[5,8,64,128]{3,2,1,0:T(8,128)S(1)} %broadcast_select_fusion.4), channel_id=1, source_target_pairs={{248,0},{0,8},{8,16},{16,24},{24,32},{32,40},{40,48},{48,56},{56,6... | collective-permute-start | bytes 3932168 | tf_op jit(solution)/shard_map/ppermute | solution.py:10
  328.0 13.8 %copy-start.2 = (f32[8,64,128]{2,1,0:T(8,128)S(1)}, f32[8,64,128]{2,1,0:T(8,128)}, u32[]{:S(2)}) copy-start(f32[8,64,128]{2,1,0:T(8,128)} %param.6) | copy-start | bytes 786436
  345.5 7.7 %collective-permute-start.6 = (f32[6,8,64,1]{2,1,3,0:T(8,128)S(1)}, f32[6,8,64,1]{2,1,3,0:T(8,128)S(1)}, u32[]{:S(2)}, u32[]{:S(2)}) collective-permute-start(f32[6,8,64,1]{2,1,3,0:T(8,128)S(1)} %copy.68), channel_id=1, source_target_pairs={{0,8},{8,16},{16,24},{24,32},{32,40},{40,48},{48,56},{56,64},{64,7... | collective-permute-start | bytes 36872 | tf_op jit(solution)/shard_map/ppermute | solution.py:20
  346.7 8.9 %collective-permute-start.7 = (f32[6,8,64,1]{2,1,3,0:T(8,128)S(1)}, f32[6,8,64,1]{2,1,3,0:T(8,128)S(1)}, u32[]{:S(2)}, u32[]{:S(2)}) collective-permute-start(f32[6,8,64,1]{2,1,3,0:T(8,128)S(1)} %copy.70), channel_id=1, source_target_pairs={{8,0},{16,8},{24,16},{32,24},{40,32},{48,40},{56,48},{64,56},{72,6... | collective-permute-start | bytes 36872 | tf_op jit(solution)/shard_map/ppermute | solution.py:21
  360.1 1.1 copy-start
  360.5 56.9 %copy-start.4 = (f32[8]{0:T(128)S(1)}, f32[8]{0:T(128)}, u32[]{:S(2)}) copy-start(f32[8]{0:T(128)} %get-tuple-element.70) | copy-start | bytes 100
  360.5 56.9 %copy-start.5 = (f32[8]{0:T(128)S(1)}, f32[8]{0:T(128)}, u32[]{:S(2)}) copy-start(f32[8]{0:T(128)} %get-tuple-element.76) | copy-start | bytes 100
  360.5 56.9 %copy-start.6 = (f32[8]{0:T(128)S(1)}, f32[8]{0:T(128)}, u32[]{:S(2)}) copy-start(f32[8]{0:T(128)} %get-tuple-element.77) | copy-start | bytes 100
  360.6 56.9 %copy-start.7 = (f32[8]{0:T(128)S(1)}, f32[8]{0:T(128)}, u32[]{:S(2)}) copy-start(f32[8]{0:T(128)} %get-tuple-element.74) | copy-start | bytes 100
  360.6 56.9 %copy-start.8 = (f32[8]{0:T(128)S(1)}, f32[8]{0:T(128)}, u32[]{:S(2)}) copy-start(f32[8]{0:T(128)} %get-tuple-element.81) | copy-start | bytes 100
  360.6 56.9 %copy-start.9 = (f32[8,1]{0,1:T(1,128)S(1)}, f32[8,1]{0,1:T(1,128)}, u32[]{:S(2)}) copy-start(f32[8,1]{0,1:T(1,128)} %get-tuple-element.11) | copy-start | bytes 100
  360.6 56.9 %copy-start.11 = (f32[8,1]{0,1:T(1,128)S(1)}, f32[8,1]{0,1:T(1,128)}, u32[]{:S(2)}) copy-start(f32[8,1]{0,1:T(1,128)} %copy-done.10) | copy-start | bytes 100
  360.6 56.9 %copy-start.13 = (f32[8,1]{0,1:T(1,128)S(1)}, f32[8,1]{0,1:T(1,128)}, u32[]{:S(2)}) copy-start(f32[8,1]{0,1:T(1,128)} %copy-done.12) | copy-start | bytes 100
  360.6 56.9 %copy-start.15 = (f32[8,1]{0,1:T(1,128)S(1)}, f32[8,1]{0,1:T(1,128)}, u32[]{:S(2)}) copy-start(f32[8,1]{0,1:T(1,128)} %copy-done.14) | copy-start | bytes 100
  360.6 56.9 %copy-start.17 = (f32[8,1]{0,1:T(1,128)S(1)}, f32[8,1]{0,1:T(1,128)}, u32[]{:S(2)}) copy-start(f32[8,1]{0,1:T(1,128)} %copy-done.16) | copy-start | bytes 100
  360.6 56.9 %copy-start.19 = (f32[8,1]{0,1:T(1,128)S(1)}, f32[8,1]{0,1:T(1,128)}, u32[]{:S(2)}) copy-start(f32[8,1]{0,1:T(1,128)} %copy-done.18) | copy-start | bytes 100
  360.6 56.9 %copy-start.20 = (f32[8,1]{0,1:T(1,128)S(1)}, f32[8,1]{0,1:T(1,128)}, u32[]{:S(2)}) copy-start(f32[8,1]{0,1:T(1,128)} %get-tuple-element.29) | copy-start | bytes 100
  360.6 56.9 %copy-start.22 = (f32[8,1]{0,1:T(1,128)S(1)}, f32[8,1]{0,1:T(1,128)}, u32[]{:S(2)}) copy-start(f32[8,1]{0,1:T(1,128)} %copy-done.21) | copy-start | bytes 100
  360.7 56.9 %copy-start.25 = (f32[8]{0:T(128)S(1)}, f32[8]{0:T(128)}, u32[]{:S(2)}) copy-start(f32[8]{0:T(128)} %multiply_bitcast_fusion.3) | copy-start | bytes 100
  360.7 56.9 %copy-start.26 = (f32[8]{0:T(128)S(1)}, f32[8]{0:T(128)}, u32[]{:S(2)}) copy-start(f32[8]{0:T(128)} %get-tuple-element.69) | copy-start | bytes 100
  360.7 56.9 %copy-start.27 = (f32[8]{0:T(128)S(1)}, f32[8]{0:T(128)}, u32[]{:S(2)}) copy-start(f32[8]{0:T(128)} %get-tuple-element.71) | copy-start | bytes 100
  360.7 56.9 %copy-start.28 = (f32[8]{0:T(128)S(1)}, f32[8]{0:T(128)}, u32[]{:S(2)}) copy-start(f32[8]{0:T(128)} %get-tuple-element.72) | copy-start | bytes 100
  360.7 56.9 %copy-start.29 = (f32[8]{0:T(128)S(1)}, f32[8]{0:T(128)}, u32[]{:S(2)}) copy-start(f32[8]{0:T(128)} %get-tuple-element.73) | copy-start | bytes 100
  360.7 56.9 %copy-start.30 = (f32[8]{0:T(128)S(1)}, f32[8]{0:T(128)}, u32[]{:S(2)}) copy-start(f32[8]{0:T(128)} %get-tuple-element.75) | copy-start | bytes 100
  360.7 56.9 %copy-start.31 = (f32[8]{0:T(128)S(1)}, f32[8]{0:T(128)}, u32[]{:S(2)}) copy-start(f32[8]{0:T(128)} %get-tuple-element.78) | copy-start | bytes 100
  360.7 56.9 %copy-start.32 = (f32[8]{0:T(128)S(1)}, f32[8]{0:T(128)}, u32[]{:S(2)}) copy-start(f32[8]{0:T(128)} %get-tuple-element.79) | copy-start | bytes 100
  360.7 56.9 %copy-start.33 = (f32[8]{0:T(128)S(1)}, f32[8]{0:T(128)}, u32[]{:S(2)}) copy-start(f32[8]{0:T(128)} %get-tuple-element.80) | copy-start | bytes 100
  360.7 56.9 %copy-start.37 = (f32[8,8,128]{2,0,1:T(8,128)S(1)}, f32[8,8,128]{2,0,1:T(8,128)}, u32[]{:S(2)}) copy-start(f32[8,8,128]{2,0,1:T(8,128)} %constant_dynamic-update-slice_fusion.7) | copy-start | bytes 98308
  360.8 56.9 %copy-start.38 = (f32[8]{0:T(128)S(1)}, f32[8]{0:T(128)}, u32[]{:S(2)}) copy-start(f32[8]{0:T(128)} %multiply_bitcast_fusion.19) | copy-start | bytes 100
  360.8 57.1 %copy-start.24 = (f32[8,1]{0,1:T(1,128)S(1)}, f32[8,1]{0,1:T(1,128)}, u32[]{:S(2)}) copy-start(f32[8,1]{0,1:T(1,128)} %copy-done.23) | copy-start | bytes 100
  360.8 57.2 %copy-start.42 = (f32[8]{0:T(128)S(1)}, f32[8]{0:T(128)}, u32[]{:S(2)}) copy-start(f32[8]{0:T(128)} %multiply_bitcast_fusion.15) | copy-start | bytes 100
  360.8 57.3 %copy-start.43 = (f32[8]{0:T(128)S(1)}, f32[8]{0:T(128)}, u32[]{:S(2)}) copy-start(f32[8]{0:T(128)} %multiply_bitcast_fusion.12) | copy-start | bytes 100
  360.8 57.3 %copy-start.41 = (f32[8]{0:T(128)S(1)}, f32[8]{0:T(128)}, u32[]{:S(2)}) copy-start(f32[8]{0:T(128)} %multiply_bitcast_fusion.9) | copy-start | bytes 100
  360.8 57.4 %copy-start.40 = (f32[8]{0:T(128)S(1)}, f32[8]{0:T(128)}, u32[]{:S(2)}) copy-start(f32[8]{0:T(128)} %multiply_bitcast_fusion.6) | copy-start | bytes 100
  360.8 57.5 %copy-start.39 = (f32[8]{0:T(128)S(1)}, f32[8]{0:T(128)}, u32[]{:S(2)}) copy-start(f32[8]{0:T(128)} %multiply_bitcast_fusion.4) | copy-start | bytes 100
  360.8 57.5 %copy-start.34 = (f32[8]{0:T(128)S(1)}, f32[8]{0:T(128)}, u32[]{:S(2)}) copy-start(f32[8]{0:T(128)} %get-tuple-element.9) | copy-start | bytes 100
  360.8 57.5 %copy-start.35 = (f32[8,1]{0,1:T(1,128)S(1)}, f32[8,1]{0,1:T(1,128)}, u32[]{:S(2)}) copy-start(f32[8,1]{0,1:T(1,128)} %get-tuple-element.12) | copy-start | bytes 100
  361.2 57.5 %slice-start = ((f32[5,8,64,128]{3,2,1,0:T(8,128)}), f32[4,8,64,128]{3,2,1,0:T(8,128)S(1)}, s32[]{:S(2)}) async-start(f32[5,8,64,128]{3,2,1,0:T(8,128)} %copy-done), calls=%async_computation.1 | async-start | bytes 2097152 | tf_op jit(solution)/shard_map/slice | solution.py:137
